TPU v7x, 32 devices: a whole 2x2x4 slice. The times are simulated.
32 devices in a mesh: row: 4 (over z), col: 8 (over y, x, core).
Axes of the slice: x: 2, y: 2, z: 4, core: 2. Of those that a mesh axis runs over, the one named last changes fastest.
Arguments:
- points: bfloat16 [2, 8192], P(None, ('row', 'col')), may hold values from 0 to 1
- noise_var: float32 [8192], P(('row', 'col')), may hold values from 0.5 to 2
- district: int32 [8192], P(('row', 'col')), may hold values from 0 to 63, never falling along the last dimension, each value on 1 to 512 neighbouring positions
- solution: float32 [32, 8192], P(None, ('row', 'col')), may hold values from -6 to 6
- residual: float32 [32, 8192], P(None, ('row', 'col')), may hold values from -44 to 44
- direction: float32 [32, 8192], P(None, ('row', 'col')), may hold values from -44 to 44
Outputs:
- new_solution: float32 [32, 8192], P(None, ('row', 'col'))
- new_residual: float32 [32, 8192], P(None, ('row', 'col'))
- new_direction: float32 [32, 8192], P(None, ('row', 'col'))
Inputs may be any that keep to these rules, and one draw needn't show every extreme that they name: Samples are ordered by district; every district holds 1 to 512 samples and one holds exactly 512.
All inputs are finite; a program needn't handle non-finite values.
Results may differ from a plain program's by a relative error of at most 0.004.
Values may be sent and summed in bfloat16 or wider, within the bound.
No kernel may reach another device: no remote copies, remote signals or barrier semaphores. Data moves between devices by JAX's collectives and lax.ppermute only.
A program may use at most 64 MiB of HBM per device.

v0:
```python
import math
import jax
import jax.numpy as jnp
from jax import lax
from jax.sharding import PartitionSpec as P

NDIST = 64
root_three = math.sqrt(3.0)
corr_range = 0.05
district_gain = 0.5


def matern_tile(left_points, right_points):
    left_vals = left_points.astype(jnp.float32)
    right_vals = right_points.astype(jnp.float32)
    delta_x = left_vals[0][:, None] - right_vals[0][None, :]
    delta_y = left_vals[1][:, None] - right_vals[1][None, :]
    scaled = root_three / corr_range * jnp.sqrt(delta_x * delta_x + delta_y * delta_y)
    return ((1.0 + scaled) * jnp.exp(-scaled)).astype(jnp.bfloat16)


def small_product(left, right):
    return jnp.dot(left, right, precision=lax.Precision.HIGHEST, preferred_element_type=jnp.float32)


def chol_solve(matrix, rhs_mat):
    factor = jnp.linalg.cholesky(matrix)
    return jax.scipy.linalg.cho_solve((factor, True), rhs_mat)


def per_device(points, noise_var, district, solution, residual, direction):
    local_count = points.shape[1]
    rhs_count = direction.shape[0]
    whole_count = local_count * lax.axis_size("row") * lax.axis_size("col")
    kernel_scale = 1.0 / (corr_range * math.sqrt(whole_count))
    labels = jnp.arange(NDIST, dtype=jnp.int32)
    onehot = (district[None, :] == labels[:, None]).astype(jnp.float32)
    local_sums = small_product(direction, onehot.T)
    local_sizes = jnp.sum(onehot, axis=1)
    local_norm = small_product(residual, residual.T)
    district_sums, sizes = lax.psum((local_sums, local_sizes), ("row", "col"))
    old_norm = lax.psum(local_norm, ("row", "col"))
    lowered = direction.astype(jnp.bfloat16)
    empty = jnp.zeros((rhs_count, local_count), jnp.float32)
    left_points = lax.all_gather(points, ("row", "col"), axis=1, tiled=True)
    left_dir = lax.all_gather(lowered, ("row", "col"), axis=1, tiled=True)
    width_now = left_points.shape[1]
    block_len = 8192

    def one_step(index_now, acc):
        part_points = lax.dynamic_slice_in_dim(left_points, index_now * block_len, block_len, 1)
        part_dir = lax.dynamic_slice_in_dim(left_dir, index_now * block_len, block_len, 1)
        return acc + jnp.dot(
            part_dir, matern_tile(part_points, points), preferred_element_type=jnp.float32
        )

    kernel_part = lax.fori_loop(0, width_now // block_len, one_step, empty)
    weights = district_sums / jnp.sqrt(sizes)[None, :]
    district_part = small_product(weights, onehot)
    image = (
        noise_var[None, :] * direction + kernel_part * kernel_scale + district_gain * district_part
    )
    local_curv = small_product(direction, image.T)
    curvature = lax.psum(local_curv, ("row", "col"))
    alpha = chol_solve(curvature, old_norm)
    new_solution = solution + small_product(alpha.T, direction)
    new_residual = residual - small_product(alpha.T, image)
    new_norm = lax.psum(small_product(new_residual, new_residual.T), ("row", "col"))
    beta = chol_solve(old_norm, new_norm)
    new_direction = new_residual + small_product(beta.T, direction)
    return (new_solution, new_residual, new_direction)


def solution(mesh):
    in_specs = (
        P(None, ("row", "col")),
        P(("row", "col")),
        P(("row", "col")),
        P(None, ("row", "col")),
        P(None, ("row", "col")),
        P(None, ("row", "col")),
    )
    out_specs = (P(None, ("row", "col")), P(None, ("row", "col")), P(None, ("row", "col")))
    return jax.shard_map(
        per_device, mesh=mesh, in_specs=in_specs, out_specs=out_specs, check_vma=False
    )
```

profile of v0, /device:TPU:14, one launch (start us, length us, event | category | flops | bytes accessed | tf_op | source)
XLA Modules:
  0.0 224.8 jit_solution(12056123770513564116)
XLA Ops:
  0.7 29.1 %all_gather.6 = bf16[2,8192]{1,0:T(2,128)(2,1)S(1)} all-gather(bf16[2,256]{1,0:T(2,128)(2,1)} %param.9), channel_id=1, replica_groups=mesh['row'=4,'col'=8] {'row','col'}, dimensions={1}, use_global_device_ids=true | all-gather | bytes 33792 | tf_op jit(solution)/shard_map/all_gather | solution.py:45
  29.8 0.8 fusion.24
  30.5 0.8 convert_element_type.21
  31.3 41.2 %all_gather.7 = bf16[32,8192]{1,0:T(8,128)(2,1)S(1)} all-gather(bf16[32,256]{1,0:T(8,128)(2,1)S(1)} %convert_element_type.21), channel_id=1, replica_groups=mesh['row'=4,'col'=8] {'row','col'}, dimensions={1}, use_global_device_ids=true | all-gather | bytes 540672 | tf_op jit(solution)/shard_map/all_gather | solution.py:46
  72.5 5.2 %fusion.4 = f32[32,256]{1,0:T(8,128)S(1)} fusion(bf16[32,8192]{1,0:T(8,128)(2,1)S(1)} %all_gather.7, f32[256]{0:T(256)S(1)} %bitcast.55, f32[8192]{0:T(1024)S(1)} %bitcast.53, f32[256]{0:T(256)S(1)} %bitcast.54, f32[8192]{0:T(1024)S(1)} %bitcast.52, f32[32,256]{1,0:T(8,128)S(1)} %copy-done, f32[256]{0:T(256)S(1)} %copy-done.5), kind=kOutput, calls=%fused_computation.10 | convolution fusion | flops 155213824 | bytes 658432 | tf_op jit(solution)/shard_map/while/body/eval_jaxpr/dot_general | solution.py:53
  77.7 0.2 convolution_bitcast_fusion
  78.0 49.4 %all-reduce.1 = (f32[32,64]{0,1:T(8,128)S(1)}, f32[64]{0:T(128)S(1)}) all-reduce(f32[32,64]{0,1:T(8,128)S(1)} %convolution_bitcast_fusion, f32[64]{0:T(128)S(1)} %convert_reduce_fusion), channel_id=1, replica_groups=mesh['row'=4,'col'=8] {'row','col'}, use_global_device_ids=true, to_apply=%region_0.0 | all-reduce | flops 2112 | bytes 16896 | tf_op jit(solution)/shard_map/psum | solution.py:41
  127.3 0.3 fusion.1
  127.8 0.2 fusion.25
  128.0 38.5 %all-reduce = (f32[32,32]{0,1:T(8,128)S(1)}, f32[32,32]{0,1:T(8,128)S(1)}) all-reduce(f32[32,32]{0,1:T(8,128)S(1)} %fusion.25, f32[32,32]{0,1:T(8,128)S(1)} %convolution_bitcast_fusion.1), channel_id=1, replica_groups=mesh['row'=4,'col'=8] {'row','col'}, use_global_device_ids=true, to_apply=%region_6.8 | all-reduce | flops 2048 | bytes 16384 | tf_op jit(solution)/shard_map/psum | solution.py:42
  166.6 2.9 %cholesky.55 = f32[32,32]{1,0:T(8,128)S(1)} custom-call(f32[32,32]{1,0:T(8,128)S(1)} %get-tuple-element.31), custom_call_target="Cholesky" | custom-call | tf_op jit(solution)/shard_map/jit(cholesky)/cholesky | solution.py:27
  169.6 0.6 compare_reduce_fusion
  170.2 0.7 fusion.9
  170.9 2.4 %custom-call.9 = f32[1,32,32]{1,2,0:T(8,128)S(1)} custom-call(f32[1,32,32]{2,1,0:T(8,128)S(1)} %fusion.9), custom_call_target="InvertDiagBlocksLowerTriangular" | custom-call | tf_op jit(solution)/shard_map/jit(_cho_solve)/triangular_solve | solution.py:28
  173.3 2.9 %cholesky.44 = f32[32,32]{1,0:T(8,128)S(1)} custom-call(f32[32,32]{1,0:T(8,128)S(1)} %get-tuple-element.32), custom_call_target="Cholesky" | custom-call | tf_op jit(solution)/shard_map/jit(cholesky)/cholesky | solution.py:27
  176.3 0.6 compare_reduce_fusion.1
  176.9 0.7 fusion.8
  177.6 2.4 %custom-call.8 = f32[1,32,32]{1,2,0:T(8,128)S(1)} custom-call(f32[1,32,32]{2,1,0:T(8,128)S(1)} %fusion.8), custom_call_target="InvertDiagBlocksLowerTriangular" | custom-call | tf_op jit(solution)/shard_map/jit(_cho_solve)/triangular_solve | solution.py:28
  180.0 0.2 fusion.17
  180.4 0.2 convolution_subtract_fusion
  180.8 41.9 %psum.39 = f32[32,32]{1,0:T(8,128)S(1)} all-reduce(f32[32,32]{1,0:T(8,128)S(1)} %fusion.26), channel_id=1, replica_groups=mesh['row'=4,'col'=8] {'row','col'}, use_global_device_ids=true, to_apply=%region_7.0 | all-reduce | flops 1024 | bytes 8192 | tf_op jit(solution)/shard_map/psum | solution.py:68
  222.7 0.2 fusion.12
  223.1 0.9 convolution_add_fusion
  223.9 0.8 convolution_add_fusion.1
  (24 shorter events, 1.0 us)
Async XLA Ops:
  0.6 71.8 %copy-start = (f32[32,256]{1,0:T(8,128)S(1)}, f32[32,256]{1,0:T(8,128)}, u32[]{:S(2)}) copy-start(f32[32,256]{1,0:T(8,128)} %param.14) | copy-start | bytes 98308
  0.6 71.8 %copy-start.5 = (f32[256]{0:T(256)S(1)}, f32[256]{0:T(256)}, u32[]{:S(2)}) copy-start(f32[256]{0:T(256)} %param.10) | copy-start | bytes 3076
  72.5 5.2 %copy-start.4 = (s32[256]{0:T(256)S(1)}, s32[256]{0:T(256)}, u32[]{:S(2)}) copy-start(s32[256]{0:T(256)} %param.11) | copy-start | bytes 3076
  72.5 55.3 %copy-start.2 = (f32[32,256]{1,0:T(8,128)S(1)}, f32[32,256]{1,0:T(8,128)}, u32[]{:S(2)}) copy-start(f32[32,256]{1,0:T(8,128)} %param.13) | copy-start | bytes 98308
  127.6 96.3 %copy-start.3 = (f32[32,256]{1,0:T(8,128)S(1)}, f32[32,256]{1,0:T(8,128)}, u32[]{:S(2)}) copy-start(f32[32,256]{1,0:T(8,128)} %param.12) | copy-start | bytes 98308
  180.7 44.1 %copy-start.1 = (f32[32,256]{1,0:T(8,128)}, f32[32,256]{1,0:T(8,128)S(1)}, u32[]{:S(2)}) copy-start(f32[32,256]{1,0:T(8,128)S(1)} %convolution_subtract_fusion) | copy-start | bytes 98308
where the time goes:
time: 225 us
  blocking collectives  200 us (89%)
  other arithmetic  14.3 us (6%)
  matrix products  8.78 us (4%)
    psum x1, blocking collectives, per_device(): district_sums, sizes = lax.psum((local_sums, local_sizes), ('row', 'col'))  49.4 us
    psum x1, blocking collectives, per_device(): lax.psum(small_product(new_residual, new_residual.T), ('row', 'col'))  41.9 us
    all_gather x1, blocking collectives, per_device(): left_dir = lax.all_gather(lowered, ('row', 'col'), axis=1, tiled=True)  41.2 us
    psum x1, blocking collectives, per_device(): old_norm = lax.psum(local_norm, ('row', 'col'))  38.5 us
    all_gather x1, blocking collectives, per_device(): left_points = lax.all_gather(points, ('row', 'col'), axis=1, tiled=True)  29.1 us
    another operation x6, other arithmetic, chol_solve(): factor = jnp.linalg.cholesky(matrix)  7.2 us
    another operation x4, other arithmetic, chol_solve(): return jax.scipy.linalg.cho_solve((factor, True), rhs_mat)  6.17 us
    dot_general x1, matrix products, one_step(): jnp.dot(part_dir, matern_tile(part_points, points), preferred_element_typ...  5.2 us

commit v1 on v0

--- a/solution.py
+++ b/solution.py
@@ -42,8 +42,13 @@
     old_norm = lax.psum(local_norm, ("row", "col"))
     lowered = direction.astype(jnp.bfloat16)
     empty = jnp.zeros((rhs_count, local_count), jnp.float32)
-    left_points = lax.all_gather(points, ("row", "col"), axis=1, tiled=True)
-    left_dir = lax.all_gather(lowered, ("row", "col"), axis=1, tiled=True)
+    left_points, left_dir = jnp.split(
+        lax.all_gather(
+            jnp.concatenate([points, lowered], axis=0), ("row", "col"), axis=1, tiled=True
+        ),
+        [points.shape[0]],
+        axis=0,
+    )
     width_now = left_points.shape[1]
     block_len = 8192
 

time: 225 us -> 189 us (0.84)
  blocking collectives: 200 us -> 162 us
    all_gather x2 -> x1, blocking collectives: 70.2 us -> 30.6 us  [per_device(): lax.all_gather(jnp.concatenate([points, lowered], axis=0), ('row', 'col')...]
where the time goes in v1:
time: 189 us; the launch traced here: 187 us
  blocking collectives  162 us (86%)
  other arithmetic  15 us (8%)
  matrix products  8.89 us (5%)
    psum x1, blocking collectives, per_device(): district_sums, sizes = lax.psum((local_sums, local_sizes), ('row', 'col'))  51.1 us
    psum x1, blocking collectives, per_device(): lax.psum(small_product(new_residual, new_residual.T), ('row', 'col'))  40.6 us
    psum x1, blocking collectives, per_device(): old_norm = lax.psum(local_norm, ('row', 'col'))  39.8 us
    all_gather x1, blocking collectives, per_device(): lax.all_gather(jnp.concatenate([points, lowered], axis=0), ('row', 'col')...  30.6 us
    another operation x6, other arithmetic, chol_solve(): factor = jnp.linalg.cholesky(matrix)  7.2 us
    another operation x4, other arithmetic, chol_solve(): return jax.scipy.linalg.cho_solve((factor, True), rhs_mat)  6.17 us
    dot_general x1, matrix products, one_step(): jnp.dot(part_dir, matern_tile(part_points, points), preferred_element_typ...  5.32 us

profile of v1, /device:TPU:14, one launch (start us, length us, event | category | flops | bytes accessed | tf_op | source)
XLA Modules:
  0.0 187.0 jit_solution(5370310908700159354)
XLA Ops:
  0.7 0.8 convert_element_type.18
  1.5 0.7 pad_maximum_fusion
  2.2 30.6 %all_gather.3 = bf16[34,8192]{1,0:T(8,128)(2,1)S(1)} all-gather(bf16[34,256]{1,0:T(8,128)(2,1)S(1)} %pad_maximum_fusion), channel_id=1, replica_groups=mesh['row'=4,'col'=8] {'row','col'}, dimensions={1}, use_global_device_ids=true | all-gather | bytes 574464 | tf_op jit(solution)/shard_map/all_gather | solution.py:46
  32.9 5.3 %fusion.3 = f32[32,256]{1,0:T(8,128)S(1)} fusion(f32[256]{0:T(256)S(1)} %bitcast.50, f32[8192]{0:T(1024)S(1)} %bitcast.48, f32[256]{0:T(256)S(1)} %bitcast.49, f32[8192]{0:T(1024)S(1)} %bitcast.47, bf16[34,8192]{1,0:T(8,128)(2,1)S(1)} %all_gather.3, f32[32,256]{1,0:T(8,128)S(1)} %copy-done, f32[256]{0:T(256)S(1)} %copy-done.6), kind=kOutput, calls=%fused_computation.9 | convolution fusion | flops 155213824 | bytes 658432 | tf_op jit(solution)/shard_map/while/body/eval_jaxpr/dot_general | solution.py:58
  38.2 0.2 convolution_bitcast_fusion
  38.5 51.1 %all-reduce.1 = (f32[32,64]{0,1:T(8,128)S(1)}, f32[64]{0:T(128)S(1)}) all-reduce(f32[32,64]{0,1:T(8,128)S(1)} %convolution_bitcast_fusion, f32[64]{0:T(128)S(1)} %convert_reduce_fusion), channel_id=1, replica_groups=mesh['row'=4,'col'=8] {'row','col'}, use_global_device_ids=true, to_apply=%region_0.0 | all-reduce | flops 2112 | bytes 16896 | tf_op jit(solution)/shard_map/psum | solution.py:41
  89.6 0.3 fusion.1
  89.9 0.2 convolution_bitcast_fusion.1
  90.1 0.2 fusion.25
  90.2 39.8 %all-reduce = (f32[32,32]{0,1:T(8,128)S(1)}, f32[32,32]{0,1:T(8,128)S(1)}) all-reduce(f32[32,32]{0,1:T(8,128)S(1)} %fusion.25, f32[32,32]{0,1:T(8,128)S(1)} %convolution_bitcast_fusion.1), channel_id=1, replica_groups=mesh['row'=4,'col'=8] {'row','col'}, use_global_device_ids=true, to_apply=%region_6.8 | all-reduce | flops 2048 | bytes 16384 | tf_op jit(solution)/shard_map/psum | solution.py:42
  130.2 2.9 %cholesky.55 = f32[32,32]{1,0:T(8,128)S(1)} custom-call(f32[32,32]{1,0:T(8,128)S(1)} %get-tuple-element.31), custom_call_target="Cholesky" | custom-call | tf_op jit(solution)/shard_map/jit(cholesky)/cholesky | solution.py:27
  133.2 0.6 compare_reduce_fusion
  133.8 0.7 fusion.9
  134.5 2.4 %custom-call.9 = f32[1,32,32]{1,2,0:T(8,128)S(1)} custom-call(f32[1,32,32]{2,1,0:T(8,128)S(1)} %fusion.9), custom_call_target="InvertDiagBlocksLowerTriangular" | custom-call | tf_op jit(solution)/shard_map/jit(_cho_solve)/triangular_solve | solution.py:28
  136.9 2.9 %cholesky.44 = f32[32,32]{1,0:T(8,128)S(1)} custom-call(f32[32,32]{1,0:T(8,128)S(1)} %get-tuple-element.32), custom_call_target="Cholesky" | custom-call | tf_op jit(solution)/shard_map/jit(cholesky)/cholesky | solution.py:27
  139.9 0.6 compare_reduce_fusion.1
  140.5 0.7 fusion.8
  141.2 2.4 %custom-call.8 = f32[1,32,32]{1,2,0:T(8,128)S(1)} custom-call(f32[1,32,32]{2,1,0:T(8,128)S(1)} %fusion.8), custom_call_target="InvertDiagBlocksLowerTriangular" | custom-call | tf_op jit(solution)/shard_map/jit(_cho_solve)/triangular_solve | solution.py:28
  143.6 0.2 fusion.17
  144.0 0.2 convolution_subtract_fusion
  144.4 40.6 %psum.39 = f32[32,32]{1,0:T(8,128)S(1)} all-reduce(f32[32,32]{1,0:T(8,128)S(1)} %fusion.26), channel_id=1, replica_groups=mesh['row'=4,'col'=8] {'row','col'}, use_global_device_ids=true, to_apply=%region_7.0 | all-reduce | flops 1024 | bytes 8192 | tf_op jit(solution)/shard_map/psum | solution.py:73
  185.0 0.2 fusion.12
  185.3 0.9 convolution_add_fusion
  186.2 0.8 convolution_add_fusion.1
  (27 shorter events, 0.9 us)
Async XLA Ops:
  0.6 32.2 %copy-start = (f32[32,256]{1,0:T(8,128)S(1)}, f32[32,256]{1,0:T(8,128)}, u32[]{:S(2)}) copy-start(f32[32,256]{1,0:T(8,128)} %param.14) | copy-start | bytes 98308
  0.6 32.2 %copy-start.4 = (bf16[2,256]{1,0:T(2,128)(2,1)S(1)}, bf16[2,256]{1,0:T(2,128)(2,1)}, u32[]{:S(2)}) copy-start(bf16[2,256]{1,0:T(2,128)(2,1)} %param.9) | copy-start | bytes 3076
  0.7 32.2 %copy-start.6 = (f32[256]{0:T(256)S(1)}, f32[256]{0:T(256)}, u32[]{:S(2)}) copy-start(f32[256]{0:T(256)} %param.10) | copy-start | bytes 3076
  32.9 5.4 %copy-start.5 = (s32[256]{0:T(256)S(1)}, s32[256]{0:T(256)}, u32[]{:S(2)}) copy-start(s32[256]{0:T(256)} %param.11) | copy-start | bytes 3076
  32.9 57.2 %copy-start.2 = (f32[32,256]{1,0:T(8,128)S(1)}, f32[32,256]{1,0:T(8,128)}, u32[]{:S(2)}) copy-start(f32[32,256]{1,0:T(8,128)} %param.13) | copy-start | bytes 98308
  38.2 148.0 %copy-start.3 = (f32[32,256]{1,0:T(8,128)S(1)}, f32[32,256]{1,0:T(8,128)}, u32[]{:S(2)}) copy-start(f32[32,256]{1,0:T(8,128)} %param.12) | copy-start | bytes 98308
  144.2 42.8 %copy-start.1 = (f32[32,256]{1,0:T(8,128)}, f32[32,256]{1,0:T(8,128)S(1)}, u32[]{:S(2)}) copy-start(f32[32,256]{1,0:T(8,128)S(1)} %convolution_subtract_fusion) | copy-start | bytes 98308
